TPU v7x, 32 devices: a whole 2x2x4 slice. The times are simulated.
32 devices in a mesh: heads: 16 (over z, y, core), width: 2 (over x).
Axes of the slice: x: 2, y: 2, z: 4, core: 2. Of those that a mesh axis runs over, the one named last changes fastest.
Arguments:
- out_grad: bfloat16 [512, 7168], P('heads', 'width'), may hold values from -24 to 24
- w_out: float32 [4096, 7168], P('heads', 'width'), may hold values from -0.09375 to 0.09375
- row_moment: float32 [4096], P('heads'), may hold values from 4 to 400
- col_moment: float32 [7168], P('width'), may hold values from 4 to 400
- queries: bfloat16 [512, 6144], P('width', 'heads'), may hold values from -240 to 240
- latent: bfloat16 [512, 512], P('width'), may hold values from -6 to 6
- key_rope: bfloat16 [512, 64], P('width'), may hold values from -4 to 4
- w_kv_up: bfloat16 [512, 8192], P(None, 'heads'), may hold values from -0.25 to 0.25
- doc_lengths: int32 [2, 4], P('width'), may hold values from 1 to 160, 256 in all within a row
Outputs:
- weight_update: float32 [4096, 7168], P('heads', 'width')
- query_grad: bfloat16 [512, 6144], P('width', 'heads')
- latent_grad: float32 [512, 576], P('width', 'heads')
- kv_up_grad: float32 [512, 8192], P('width', 'heads')
Inputs may be any that keep to these rules, and one draw needn't show every extreme that they name: `doc_lengths`: row p holds the lengths of the 4 documents packed in order into pack p; they sum to 256 and the longest in every row is exactly 160.
All inputs are finite; a program needn't handle non-finite values.
Results may differ from a plain program's by a relative error of at most 0.0088.
Values may be sent and summed in bfloat16 or wider, within the bound.
No kernel may reach another device: no remote copies, remote signals or barrier semaphores. Data moves between devices by JAX's collectives and lax.ppermute only.
A program may use at most 64 MiB of HBM per device.

v0:
```python
import jax
import jax.numpy as jnp
from jax import lax
from jax.sharding import PartitionSpec as P

D = 7168
VD = 128
NOPE = 128
ROPE = 64
moment_decay = 0.9
update_eps = 1e-06


def doc_mask(lengths, length):
    doc_ends = jnp.cumsum(lengths)
    position = jnp.arange(length, dtype=jnp.int32)
    document = jnp.sum((position[:, None] >= doc_ends[None, :]).astype(jnp.int32), axis=1)
    return (document[:, None] == document[None, :]) & (position[None, :] <= position[:, None])


def forward_pack(queries, latent, key_rope, w_kv_up, allowed):
    length = queries.shape[0]
    n_heads = w_kv_up.shape[1] // (NOPE + VD)
    scale_factor = (NOPE + ROPE) ** (-0.5)
    key_value = jnp.dot(latent, w_kv_up, preferred_element_type=jnp.float32).astype(jnp.bfloat16)
    key_value = key_value.reshape(length, n_heads, NOPE + VD)
    key_nope = key_value[:, :, :NOPE]
    values = key_value[:, :, NOPE:]
    query_heads = queries.reshape(length, n_heads, NOPE + ROPE)
    scores = jnp.einsum(
        "ihd,jhd->hij", query_heads[:, :, :NOPE], key_nope, preferred_element_type=jnp.float32
    )
    scores = scores + jnp.einsum(
        "ihd,jd->hij", query_heads[:, :, NOPE:], key_rope, preferred_element_type=jnp.float32
    )
    scores = scores * scale_factor
    masked = jnp.where(allowed[None], scores, -jnp.inf)
    highest = jnp.max(masked, axis=2, keepdims=True)
    weights = jnp.exp(masked - highest)
    prob_full = weights / jnp.sum(weights, axis=2, keepdims=True)
    probs_half = prob_full.astype(jnp.bfloat16)
    attended = jnp.einsum("hij,jhd->ihd", probs_half, values, preferred_element_type=jnp.float32)
    attended = attended.astype(jnp.bfloat16).reshape(length, n_heads * VD)
    return (query_heads, key_nope, values, prob_full, probs_half, attended)


def backward_pack(states, attn_half, key_rope, w_kv_up):
    query_heads, key_nope, values, prob_full, probs_half, attended = states
    length = query_heads.shape[0]
    n_heads = query_heads.shape[1]
    scale_factor = (NOPE + ROPE) ** (-0.5)
    grad_heads = attn_half.reshape(length, n_heads, VD)
    row_delta = jnp.sum(
        grad_heads.astype(jnp.float32) * attended.reshape(length, n_heads, VD).astype(jnp.float32),
        axis=2,
    ).T
    prob_grad = jnp.einsum("ihd,jhd->hij", grad_heads, values, preferred_element_type=jnp.float32)
    score_grad = (prob_full * (prob_grad - row_delta[:, :, None]) * scale_factor).astype(
        jnp.bfloat16
    )
    nope_grad = jnp.einsum("hij,jhd->ihd", score_grad, key_nope, preferred_element_type=jnp.float32)
    rotary_grad = jnp.einsum(
        "hij,jd->ihd", score_grad, key_rope, preferred_element_type=jnp.float32
    )
    query_grad = jnp.concatenate([nope_grad, rotary_grad], axis=2).astype(jnp.bfloat16)
    query_grad = query_grad.reshape(length, n_heads * (NOPE + ROPE))
    key_nope_grad = jnp.einsum(
        "hij,ihd->jhd", score_grad, query_heads[:, :, :NOPE], preferred_element_type=jnp.float32
    )
    rope_grad = jnp.einsum(
        "hij,ihd->jd", score_grad, query_heads[:, :, NOPE:], preferred_element_type=jnp.float32
    )
    value_grad = jnp.einsum(
        "hij,ihd->jhd", probs_half, grad_heads, preferred_element_type=jnp.float32
    )
    kv_grad = jnp.concatenate([key_nope_grad, value_grad], axis=2).astype(jnp.bfloat16)
    kv_grad = kv_grad.reshape(length, n_heads * (NOPE + VD))
    latent_part = lax.dot_general(
        kv_grad, w_kv_up, (((1,), (1,)), ((), ())), preferred_element_type=jnp.float32
    )
    latent_term = jnp.concatenate([latent_part, rope_grad], axis=1)
    return (query_grad, latent_term, kv_grad)


def on_device(
    out_grad, w_out, row_moment, col_moment, queries, latent, key_rope, w_kv_up, doc_lengths
):
    length = queries.shape[0]
    allowed = doc_mask(doc_lengths[0], length)
    states = forward_pack(queries, latent, key_rope, w_kv_up, allowed)
    attended = states[5]
    w_half = w_out.astype(jnp.bfloat16)
    grad_rows = lax.all_gather(out_grad, "heads", axis=0, tiled=True)
    picked = grad_rows
    attn_grad = lax.psum_scatter(
        lax.dot_general(
            picked, w_half, (((1,), (1,)), ((), ())), preferred_element_type=jnp.float32
        ),
        "width",
        scatter_dimension=0,
        tiled=True,
    )
    attn_half = attn_grad.astype(jnp.bfloat16)
    picked = grad_rows
    gradient = lax.dot_general(
        lax.all_gather(attended, "width", axis=0, tiled=True),
        picked,
        (((0,), (0,)), ((), ())),
        preferred_element_type=jnp.float32,
    )
    query_grad, latent_term, kv_grad = backward_pack(states, attn_half, key_rope, w_kv_up)
    latent_grad = lax.psum_scatter(latent_term, "heads", scatter_dimension=1, tiled=True)
    picked = latent
    kv_up_grad = lax.psum_scatter(
        lax.dot_general(
            picked, kv_grad, (((0,), (0,)), ((), ())), preferred_element_type=jnp.float32
        ),
        "width",
        scatter_dimension=0,
        tiled=True,
    )
    squares = gradient * gradient
    row_part = jnp.sum(squares, axis=1)
    col_part = jnp.sum(squares, axis=0)
    row_count = gradient.shape[0]
    col_count = gradient.shape[1]
    rows_total = row_count * lax.axis_size("heads")
    head_index = lax.axis_index("heads")
    width_index = lax.axis_index("width")
    row_full = lax.dynamic_update_slice(
        jnp.zeros((rows_total,), jnp.float32), row_part, (head_index * row_count,)
    )
    col_full = lax.dynamic_update_slice(
        jnp.zeros((D,), jnp.float32), col_part, (width_index * col_count,)
    )
    row_all, col_all = lax.psum((row_full, col_full), ("heads", "width"))
    row_sum = lax.dynamic_slice_in_dim(row_all, head_index * row_count, row_count, 0)
    col_sum = lax.dynamic_slice_in_dim(col_all, width_index * col_count, col_count, 0)
    row_new = moment_decay * row_moment + (1.0 - moment_decay) * row_sum / D
    col_new = moment_decay * col_moment + (1.0 - moment_decay) * col_sum / rows_total
    scaled = gradient / jnp.sqrt(row_new[:, None] * col_new[None, :])
    mean_square = lax.psum(jnp.sum(scaled * scaled), ("heads", "width")) / (rows_total * D)
    weight_update = scaled / jnp.sqrt(mean_square + update_eps)
    return (weight_update, query_grad, latent_grad, kv_up_grad)


def solution(mesh):
    in_specs = (
        P("heads", "width"),
        P("heads", "width"),
        P("heads"),
        P("width"),
        P("width", "heads"),
        P("width", None),
        P("width", None),
        P(None, "heads"),
        P("width", None),
    )
    out_specs = (P("heads", "width"), P("width", "heads"), P("width", "heads"), P("width", "heads"))
    return jax.shard_map(
        on_device, mesh=mesh, in_specs=in_specs, out_specs=out_specs, check_vma=False
    )
```

profile of v0, /device:TPU:0, one launch (start us, length us, event | category | flops | bytes accessed | tf_op | source)
XLA Modules:
  0.0 205.8 jit_solution(9484889876110462075)
XLA Ops:
  7.2 0.7 all-gather.2.cloned.1.call-update
  8.0 1.1 copy.75
  9.0 1.2 convolution_convert_fusion
  10.7 0.8 reduce-window.8
  11.5 1.2 dynamic-slice
  12.8 47.9 %all-gather.2.cloned.1.call-done = bf16[512,3584]{1,0:T(8,128)(2,1)} async-done(((bf16[32,3584]{1,0:T(8,128)(2,1)}), bf16[512,3584]{1,0:T(8,128)(2,1)}) %all-gather.2.cloned.1.call-update) | async-done | bytes 3670032 | tf_op jit(solution)/shard_map/all_gather | solution.py:93
  60.7 5.1 %fusion.2 = f32[512,256]{1,0:T(8,128)} fusion(bf16[512,3584]{1,0:T(8,128)(2,1)} %all-gather.2.cloned.1.call-done, f32[256,3584]{1,0:T(8,128)} %param.10), kind=kOutput, calls=%fused_computation.6 | convolution fusion | flops 940441600 | bytes 7864320 | tf_op jit(solution)/shard_map/dot_general | solution.py:96
  66.3 0.3 fusion.10
  66.5 0.4 fusion.29
  66.9 12.4 %reduce-scatter.4.cloned.1.call-done = f32[256,256]{1,0:T(8,128)} async-done(((f32[512,256]{1,0:T(8,128)}), f32[256,256]{1,0:T(8,128)}) %reduce-scatter.4.cloned.1.call-update) | async-done | bytes 262160 | tf_op jit(solution)/shard_map/reduce_scatter | solution.py:95
  79.3 1.0 convert_element_type.46
  80.4 0.3 multiply_reduce_fusion.3
  80.7 0.3 fusion.14
  81.0 0.3 fusion.11
  81.2 0.2 fusion.13
  81.7 0.3 fusion.30
  82.1 0.9 pad_maximum_fusion
  83.0 5.7 %all_gather.6 = bf16[512,256]{0,1:T(8,128)(2,1)S(1)} all-gather(bf16[256,256]{0,1:T(8,128)(2,1)S(1)} %bitcast.69), channel_id=1, replica_groups=mesh['heads'=16,'width'=2] {'width'}, dimensions={0}, use_global_device_ids=true | all-gather | bytes 393216 | tf_op jit(solution)/shard_map/all_gather | solution.py:106
  88.8 5.1 %multiply_reduce_fusion.2 = (f32[256]{0:T(256)S(1)}, f32[3584]{0:T(1024)S(1)}, f32[256,3584]{1,0:T(8,128)}) fusion(bf16[512,256]{0,1:T(8,128)(2,1)S(1)} %all_gather.6, bf16[512,3584]{1,0:T(8,128)(2,1)} %all-gather.2.cloned.1.call-done), kind=kOutput, calls=%fused_computation.4 | convolution fusion | flops 942272768 | bytes 7617536 | tf_op jit(solution)/shard_map/dot_general | solution.py:105
  93.8 0.3 dynamic_update_slice.7
  94.2 0.3 dynamic_update_slice.6
  94.5 40.0 %all-reduce.1 = (f32[7168]{0:T(1024)S(1)}, f32[4096]{0:T(1024)S(1)}) all-reduce(f32[7168]{0:T(1024)S(1)} %dynamic_update_slice.7, f32[4096]{0:T(1024)S(1)} %dynamic_update_slice.6), channel_id=1, replica_groups=mesh['heads'=16,'width'=2] {'heads','width'}, use_global_device_ids=true, to_apply=%region_7.8 | all-reduce | flops 11264 | bytes 90112 | tf_op jit(solution)/shard_map/psum | solution.py:136
  134.6 1.3 convolution_bitcast_fusion
  136.0 3.7 %multiply_reduce_fusion = f32[]{:T(128)} fusion(f32[256,3584]{1,0:T(8,128)} %get-tuple-element.28, f32[3584]{0:T(1024)S(1)} %multiply_add_fusion, f32[256]{0:T(256)S(1)} %multiply_add_fusion.1), kind=kLoop, calls=%fused_computation.1 | loop fusion | flops 3670015 | bytes 3685380 | tf_op jit(solution)/shard_map/reduce_sum | solution.py:142
  140.3 41.3 %psum.23 = f32[]{:T(128)} all-reduce(f32[]{:T(128)} %multiply_reduce_fusion), channel_id=1, replica_groups=mesh['heads'=16,'width'=2] {'heads','width'}, use_global_device_ids=true, to_apply=%region_9.10 | all-reduce | flops 1 | bytes 8 | tf_op jit(solution)/shard_map/psum | solution.py:142
  181.7 0.2 fusion.12
  182.0 0.8 copy.90
  183.5 4.4 %fusion.1 = f32[256,3584]{1,0:T(8,128)} fusion(f32[256,3584]{1,0:T(8,128)} %get-tuple-element.28, f32[]{:T(128)S(6)} %sqrt.7, f32[3584]{0:T(1024)S(1)} %multiply_add_fusion, f32[256]{0:T(256)S(1)} %multiply_add_fusion.1), kind=kLoop, calls=%fused_computation.5 | loop fusion | flops 2752512 | bytes 7355396 | tf_op jit(solution)/shard_map/div | solution.py:143
  187.9 1.0 constant_dynamic-slice_fusion
  189.0 0.7 copy.91
  189.7 7.6 %reduce-scatter.6.cloned.1.call-done = f32[256,512]{0,1:T(8,128)} async-done(((f32[512,512]{0,1:T(8,128)}), f32[256,512]{0,1:T(8,128)}) %reduce-scatter.6.cloned.1.call-update) | async-done | bytes 524304 | tf_op jit(solution)/shard_map/reduce_scatter | solution.py:114
  197.2 2.0 copy.92
  (33 shorter events, 1.7 us)
Async XLA Ops:
  7.2 1.9 copy-start
  7.2 53.5 %all-gather.2.cloned.1.call-start = ((), (), s32[]{:S(2)}) async-start(), calls=%async_computation.2 | async-start | bytes 3899392 | tf_op jit(solution)/shard_map/all_gather | solution.py:93
  7.9 71.4 %reduce-scatter.4.cloned.1.call-start = ((), (), s32[]{:S(2)}) async-start(), calls=%async_computation.3 | async-start | bytes 786432 | tf_op jit(solution)/shard_map/reduce_scatter | solution.py:95
  12.8 53.5 %copy-start.2 = (bf16[256,64]{0,1:T(8,128)(2,1)S(1)}, bf16[256,64]{0,1:T(8,128)(2,1)}, u32[]{:S(2)}) copy-start(bf16[256,64]{0,1:T(8,128)(2,1)} %param.15) | copy-start | bytes 98308
  65.8 122.1 %all-reduce.4.cloned.1.call-start = ((), (), s32[]{:S(2)}) async-start(), calls=%async_computation.5 | async-start | bytes 1310720
  83.0 114.3 %reduce-scatter.6.cloned.1.call-start = ((), (), s32[]{:S(2)}) async-start(), calls=%async_computation.4 | async-start | bytes 1572864 | tf_op jit(solution)/shard_map/reduce_scatter | solution.py:114
  88.8 45.7 %copy-start.3 = (f32[3584]{0:T(1024)S(1)}, f32[3584]{0:T(1024)}, u32[]{:S(2)}) copy-start(f32[3584]{0:T(1024)} %param.12) | copy-start | bytes 43012
  88.8 45.8 %copy-start.4 = (f32[256]{0:T(256)S(1)}, f32[256]{0:T(256)}, u32[]{:S(2)}) copy-start(f32[256]{0:T(256)} %param.11) | copy-start | bytes 3076
  88.8 45.9 %copy-start.1 = (bf16[256,512]{1,0:T(8,128)(2,1)S(1)}, bf16[256,512]{1,0:T(8,128)(2,1)}, u32[]{:S(2)}) copy-start(bf16[256,512]{1,0:T(8,128)(2,1)} %param.14) | copy-start | bytes 786436
Sparse Core Ops, SparseCore 0:
  10.3 50.3 all-gather.1
  65.9 13.3 reduce-scatter.3
  83.1 91.8 all-reduce.3
  177.1 20.1 reduce-scatter.5
where the time goes:
time: 206 us
  blocking collectives  87 us (42%)
  waiting for transfers between devices  68.6 us (33%)
  between operations  15.3 us (7%)
  matrix products  15.2 us (7%)
  other arithmetic  11.6 us (6%)
  local copies, waits for them, and re-layouts  8.01 us (4%)
    all_gather x1, waiting for transfers between devices, on_device(): grad_rows = lax.all_gather(out_grad, 'heads', axis=0, tiled=True)  47.9 us
    psum x1, blocking collectives, on_device(): lax.psum(jnp.sum(scaled * scaled), ('heads', 'width')) / (rows_total * D)  41.3 us
    psum x1, blocking collectives, on_device(): row_all, col_all = lax.psum((row_full, col_full), ('heads', 'width'))  40 us
    reduce_scatter x1, waiting for transfers between devices, on_device(): lax.psum_scatter(lax.dot_general(picked, w_half, (((1,), (1,)), ((), ()))...  12.4 us
    reduce_scatter x1, waiting for transfers between devices, on_device(): lax.psum_scatter(lax.dot_general(picked, kv_grad, (((0,), (0,)), ((), ())...  7.56 us
    unnamed x17, local copies, waits for them, and re-layouts  7.03 us
    all_gather x1, blocking collectives, on_device(): lax.all_gather(attended, 'width', axis=0, tiled=True)  5.74 us
    dot_general x1, matrix products, on_device(): lax.dot_general(picked, w_half, (((1,), (1,)), ((), ())), preferred_eleme...  5.1 us
  transfers between devices with their start and end apart: 4, of which 3 were waited for; matrix products, arithmetic and copies ran while one was open for 12% of the time, Pallas kernels for 0%

commit v1 on v0

--- a/solution.py
+++ b/solution.py
@@ -90,7 +90,24 @@
     states = forward_pack(queries, latent, key_rope, w_kv_up, allowed)
     attended = states[5]
     w_half = w_out.astype(jnp.bfloat16)
-    grad_rows = lax.all_gather(out_grad, "heads", axis=0, tiled=True)
+
+    def drive_leaf(vector):
+        across = "heads"
+        chips = lax.psum(1, axis_name=across)
+        seen = tuple(((w, (w + 1) % chips) for w in range(chips)))
+        sheets = tuple(((w, (w - 1) % chips) for w in range(chips)))
+        newest, odd = ([vector], [vector])
+        for _ in range(chips // 2):
+            vec_out = lax.ppermute(newest[-1], axis_name=across, perm=seen)
+            newest.append(vec_out)
+        for _ in range((chips - 1) // 2):
+            odd.append(lax.ppermute(odd[-1], axis_name=across, perm=sheets))
+        even = jnp.concatenate([*newest[::-1], *odd[1:]], 0)
+        d_next = lax.axis_index(across)
+        after = jnp.roll(even, (d_next - chips // 2) * vector.shape[0], 0)
+        return after
+
+    grad_rows = drive_leaf(out_grad)
     picked = grad_rows
     attn_grad = lax.psum_scatter(
         lax.dot_general(

time: 206 us -> 233 us (1.13)
  starting transfers between devices: 0.16 us -> 32.4 us
  waiting for transfers between devices: 68.6 us -> 49.6 us
  local copies, waits for them, and re-layouts: 8.01 us -> 23.7 us
  matrix products: 15.2 us -> 12 us
    all_gather x1 -> x0, waiting for transfers between devices: 47.9 us -> none  [on_device(): grad_rows = lax.all_gather(out_grad, 'heads', axis=0, tiled=True)]
    ppermute x0 -> x15, starting transfers between devices: none -> 32.3 us  [the longest x7 31.7 us: drive_leaf(): odd.append(lax.ppermute(odd[-1], axis_name=across, perm=sheets))]
    ppermute x0 -> x15, waiting for transfers between devices: none -> 29.6 us  [the longest x8 29.4 us: drive_leaf(): vec_out = lax.ppermute(newest[-1], axis_name=across, perm=seen)]
    unnamed x17 -> x60, local copies, waits for them, and re-layouts: 7.03 us -> 22.6 us
    dot_general x1, matrix products: 5.1 us -> 1.94 us  [on_device(): lax.dot_general(picked, w_half, (((1,), (1,)), ((), ())), preferred_eleme...]
  transfers between devices with their start and end apart: 4 -> 18, of which waited for: 3 -> 11; matrix products, arithmetic and copies ran while one was open for 12% -> 13% of each run, Pallas kernels for 0% -> 0%
where the time goes in v1:
time: 233 us; the launch traced here: 232 us
  blocking collectives  87.3 us (37%)
  waiting for transfers between devices  49.6 us (21%)
  starting transfers between devices  32.4 us (14%)
  local copies, waits for them, and re-layouts  23.7 us (10%)
  between operations  15.7 us (7%)
  matrix products  12 us (5%)
  other arithmetic  11.8 us (5%)
    psum x1, blocking collectives, on_device(): lax.psum(jnp.sum(scaled * scaled), ('heads', 'width')) / (rows_total * D)  41.6 us
    psum x1, blocking collectives, on_device(): row_all, col_all = lax.psum((row_full, col_full), ('heads', 'width'))  40 us
    ppermute x7, starting transfers between devices, drive_leaf(): odd.append(lax.ppermute(odd[-1], axis_name=across, perm=sheets))  31.7 us
    ppermute x8, waiting for transfers between devices, drive_leaf(): vec_out = lax.ppermute(newest[-1], axis_name=across, perm=seen)  29.4 us
    unnamed x60, local copies, waits for them, and re-layouts  22.6 us
    reduce_scatter x1, waiting for transfers between devices, on_device(): lax.psum_scatter(lax.dot_general(picked, w_half, (((1,), (1,)), ((), ()))...  11.4 us
    reduce_scatter x1, waiting for transfers between devices, on_device(): lax.psum_scatter(lax.dot_general(picked, kv_grad, (((0,), (0,)), ((), ())...  8.52 us
    all_gather x1, blocking collectives, on_device(): lax.all_gather(attended, 'width', axis=0, tiled=True)  5.76 us
  transfers between devices with their start and end apart: 18, of which 11 were waited for; matrix products, arithmetic and copies ran while one was open for 13% of the time, Pallas kernels for 0%

profile of v1, /device:TPU:0, one launch (start us, length us, event | category | flops | bytes accessed | tf_op | source)
XLA Modules:
  0.0 232.3 jit_solution(9840674544002927317)
XLA Ops:
  7.8 8.9 %collective-permute-done = bf16[32,3584]{1,0:T(8,128)(2,1)S(1)} collective-permute-done((bf16[32,3584]{1,0:T(8,128)(2,1)}, bf16[32,3584]{1,0:T(8,128)(2,1)S(1)}, u32[]{:S(2)}, u32[]{:S(2)}) %collective-permute-start) | collective-permute-done | bytes 229408 | tf_op jit(solution)/shard_map/ppermute | solution.py:101
  16.7 4.4 %collective-permute-start.8 = (bf16[32,3584]{1,0:T(8,128)(2,1)}, bf16[32,3584]{1,0:T(8,128)(2,1)S(1)}, u32[]{:S(2)}, u32[]{:S(2)}) collective-permute-start(bf16[32,3584]{1,0:T(8,128)(2,1)} %param.9), channel_id=1, source_target_pairs={{0,30},{2,0},{4,2},{6,4},{8,6},{10,8},{12,10},{14,12},{16,14},{18,... | collective-permute-start | bytes 688136 | tf_op jit(solution)/shard_map/ppermute | solution.py:104
  21.1 3.7 %collective-permute-done.1 = bf16[32,3584]{1,0:T(8,128)(2,1)S(1)} collective-permute-done((bf16[32,3584]{1,0:T(8,128)(2,1)S(1)}, bf16[32,3584]{1,0:T(8,128)(2,1)S(1)}, u32[]{:S(2)}, u32[]{:S(2)}) %collective-permute-start.1) | collective-permute-done | bytes 229408 | tf_op jit(solution)/shard_map/ppermute | solution.py:101
  25.0 4.6 %collective-permute-start.9 = (bf16[32,3584]{1,0:T(8,128)(2,1)S(1)}, bf16[32,3584]{1,0:T(8,128)(2,1)S(1)}, u32[]{:S(2)}, u32[]{:S(2)}) collective-permute-start(bf16[32,3584]{1,0:T(8,128)(2,1)S(1)} %collective-permute-done.8), channel_id=1, source_target_pairs={{0,30},{2,0},{4,2},{6,4},{8,6},{10,8},{12,10},{14,12},{16,14},{18,... | collective-permute-start | bytes 688136 | tf_op jit(solution)/shard_map/ppermute | solution.py:104
  29.6 3.5 %collective-permute-done.2 = bf16[32,3584]{1,0:T(8,128)(2,1)S(1)} collective-permute-done((bf16[32,3584]{1,0:T(8,128)(2,1)S(1)}, bf16[32,3584]{1,0:T(8,128)(2,1)S(1)}, u32[]{:S(2)}, u32[]{:S(2)}) %collective-permute-start.2) | collective-permute-done | bytes 229408 | tf_op jit(solution)/shard_map/ppermute | solution.py:101
  33.1 4.7 %collective-permute-start.10 = (bf16[32,3584]{1,0:T(8,128)(2,1)S(1)}, bf16[32,3584]{1,0:T(8,128)(2,1)S(1)}, u32[]{:S(2)}, u32[]{:S(2)}) collective-permute-start(bf16[32,3584]{1,0:T(8,128)(2,1)S(1)} %collective-permute-done.9), channel_id=1, source_target_pairs={{0,30},{2,0},{4,2},{6,4},{8,6},{10,8},{12,10},{14,12},{16,14},{18,... | collective-permute-start | bytes 688136 | tf_op jit(solution)/shard_map/ppermute | solution.py:104
  37.8 3.5 %collective-permute-done.3 = bf16[32,3584]{1,0:T(8,128)(2,1)S(1)} collective-permute-done((bf16[32,3584]{1,0:T(8,128)(2,1)S(1)}, bf16[32,3584]{1,0:T(8,128)(2,1)S(1)}, u32[]{:S(2)}, u32[]{:S(2)}) %collective-permute-start.3) | collective-permute-done | bytes 229408 | tf_op jit(solution)/shard_map/ppermute | solution.py:101
  41.4 4.7 %collective-permute-start.11 = (bf16[32,3584]{1,0:T(8,128)(2,1)S(1)}, bf16[32,3584]{1,0:T(8,128)(2,1)S(1)}, u32[]{:S(2)}, u32[]{:S(2)}) collective-permute-start(bf16[32,3584]{1,0:T(8,128)(2,1)S(1)} %collective-permute-done.10), channel_id=1, source_target_pairs={{0,30},{2,0},{4,2},{6,4},{8,6},{10,8},{12,10},{14,12},{16,14},{18,... | collective-permute-start | bytes 688136 | tf_op jit(solution)/shard_map/ppermute | solution.py:104
  46.1 3.5 %collective-permute-done.4 = bf16[32,3584]{1,0:T(8,128)(2,1)S(1)} collective-permute-done((bf16[32,3584]{1,0:T(8,128)(2,1)S(1)}, bf16[32,3584]{1,0:T(8,128)(2,1)S(1)}, u32[]{:S(2)}, u32[]{:S(2)}) %collective-permute-start.4) | collective-permute-done | bytes 229408 | tf_op jit(solution)/shard_map/ppermute | solution.py:101
  49.6 1.1 copy.75
  50.7 4.4 %collective-permute-start.12 = (bf16[32,3584]{1,0:T(8,128)(2,1)S(1)}, bf16[32,3584]{1,0:T(8,128)(2,1)}, u32[]{:S(2)}, u32[]{:S(2)}) collective-permute-start(bf16[32,3584]{1,0:T(8,128)(2,1)S(1)} %collective-permute-done.11), channel_id=1, source_target_pairs={{0,30},{2,0},{4,2},{6,4},{8,6},{10,8},{12,10},{14,12},{16,14},{18,... | collective-permute-start | bytes 688136 | tf_op jit(solution)/shard_map/ppermute | solution.py:104
  55.1 2.8 %collective-permute-done.5 = bf16[32,3584]{1,0:T(8,128)(2,1)} collective-permute-done((bf16[32,3584]{1,0:T(8,128)(2,1)S(1)}, bf16[32,3584]{1,0:T(8,128)(2,1)}, u32[]{:S(2)}, u32[]{:S(2)}) %collective-permute-start.5) | collective-permute-done | bytes 229408 | tf_op jit(solution)/shard_map/ppermute | solution.py:101
  57.9 1.2 convolution_convert_fusion
  60.1 4.4 %collective-permute-start.13 = (bf16[32,3584]{1,0:T(8,128)(2,1)}, bf16[32,3584]{1,0:T(8,128)(2,1)}, u32[]{:S(2)}, u32[]{:S(2)}) collective-permute-start(bf16[32,3584]{1,0:T(8,128)(2,1)} %collective-permute-done.12), channel_id=1, source_target_pairs={{0,30},{2,0},{4,2},{6,4},{8,6},{10,8},{12,10},{14,12},{16,14},{18,... | collective-permute-start | bytes 688136 | tf_op jit(solution)/shard_map/ppermute | solution.py:104
  64.6 1.8 collective-permute-done.6
  67.3 1.3 dynamic-slice
  68.6 4.4 %collective-permute-start.14 = (bf16[32,3584]{1,0:T(8,128)(2,1)}, bf16[32,3584]{1,0:T(8,128)(2,1)S(1)}, u32[]{:S(2)}, u32[]{:S(2)}) collective-permute-start(bf16[32,3584]{1,0:T(8,128)(2,1)} %collective-permute-done.13), channel_id=1, source_target_pairs={{0,30},{2,0},{4,2},{6,4},{8,6},{10,8},{12,10},{14,12},{16,14},{18,... | collective-permute-start | bytes 688136 | tf_op jit(solution)/shard_map/ppermute | solution.py:104
  73.1 1.7 collective-permute-done.7
  86.9 3.0 %copy-done.1 = bf16[1024,3584]{1,0:T(8,128)(2,1)} copy-done((bf16[1024,3584]{1,0:T(8,128)(2,1)}, bf16[1024,3584]{1,0:T(8,128)(2,1)S(1)}, u32[]{:S(2)}) %copy-start.1) | copy-done | bytes 7340056
  89.8 1.9 fusion.1
  92.9 11.4 %reduce-scatter.4.cloned.1.call-done = f32[256,256]{1,0:T(8,128)} async-done(((f32[512,256]{1,0:T(8,128)}), f32[256,256]{1,0:T(8,128)}) %reduce-scatter.4.cloned.1.call-update) | async-done | bytes 262160 | tf_op jit(solution)/shard_map/reduce_scatter | solution.py:112
  104.3 1.0 convert_element_type.46
  106.6 1.3 convolution_bitcast_fusion
  109.4 5.8 %all_gather.3 = bf16[512,256]{0,1:T(8,128)(2,1)S(1)} all-gather(bf16[256,256]{0,1:T(8,128)(2,1)S(1)} %bitcast.67), channel_id=1, replica_groups=mesh['heads'=16,'width'=2] {'width'}, dimensions={0}, use_global_device_ids=true | all-gather | bytes 393216 | tf_op jit(solution)/shard_map/all_gather | solution.py:123
  115.2 5.0 %multiply_reduce_fusion.2 = (f32[256]{0:T(256)S(1)}, f32[3584]{0:T(1024)S(1)}, f32[256,3584]{1,0:T(8,128)}) fusion(bf16[512,256]{0,1:T(8,128)(2,1)S(1)} %all_gather.3, bf16[1024,3584]{1,0:T(8,128)(2,1)} %copy-done.1, s32[]{:T(128)S(6)} %select_n.27), kind=kOutput, calls=%fused_computation.4 | convolution fusion | flops 942272768 | bytes 7617540 | tf_op jit(solution)/shard_map/dot_general | solution.py:122
  120.9 40.0 %all-reduce.1 = (f32[7168]{0:T(1024)S(1)}, f32[4096]{0:T(1024)S(1)}) all-reduce(f32[7168]{0:T(1024)S(1)} %dynamic_update_slice.7, f32[4096]{0:T(1024)S(1)} %dynamic_update_slice.6), channel_id=1, replica_groups=mesh['heads'=16,'width'=2] {'heads','width'}, use_global_device_ids=true, to_apply=%region_7.8 | all-reduce | flops 11264 | bytes 90112 | tf_op jit(solution)/shard_map/psum | solution.py:153
  161.0 3.7 %multiply_reduce_fusion = f32[]{:T(128)} fusion(f32[256,3584]{1,0:T(8,128)} %get-tuple-element.28, f32[3584]{0:T(1024)S(1)} %multiply_add_fusion, f32[256]{0:T(256)S(1)} %multiply_add_fusion.1), kind=kLoop, calls=%fused_computation.1 | loop fusion | flops 3670015 | bytes 3685380 | tf_op jit(solution)/shard_map/reduce_sum | solution.py:159
  165.4 41.6 %psum.23 = f32[]{:T(128)} all-reduce(f32[]{:T(128)} %multiply_reduce_fusion), channel_id=1, replica_groups=mesh['heads'=16,'width'=2] {'heads','width'}, use_global_device_ids=true, to_apply=%region_9.10 | all-reduce | flops 1 | bytes 8 | tf_op jit(solution)/shard_map/psum | solution.py:159
  208.9 4.6 %fusion.5 = f32[256,3584]{1,0:T(8,128)} fusion(f32[256,3584]{1,0:T(8,128)} %get-tuple-element.28, f32[]{:T(128)S(6)} %sqrt.7, f32[3584]{0:T(1024)S(1)} %multiply_add_fusion, f32[256]{0:T(256)S(1)} %multiply_add_fusion.1), kind=kLoop, calls=%fused_computation.9 | loop fusion | flops 2752512 | bytes 7355396 | tf_op jit(solution)/shard_map/div | solution.py:160
  213.5 1.0 constant_dynamic-slice_fusion
  215.3 8.5 %reduce-scatter.6.cloned.1.call-done = f32[256,512]{0,1:T(8,128)} async-done(((f32[512,512]{0,1:T(8,128)}), f32[256,512]{0,1:T(8,128)}) %reduce-scatter.6.cloned.1.call-update) | async-done | bytes 524304 | tf_op jit(solution)/shard_map/reduce_scatter | solution.py:131
  223.8 2.0 copy.92
  (104 shorter events, 21.2 us)
Async XLA Ops:
  7.2 50.7 %copy-start = (bf16[512,512]{1,0:T(8,128)(2,1)S(1)}, bf16[512,512]{1,0:T(8,128)(2,1)}, u32[]{:S(2)}) copy-start(bf16[512,512]{1,0:T(8,128)(2,1)} %param.16) | copy-start | bytes 1572868
  7.2 77.6 %copy-start.3 = (bf16[32,3584]{1,0:T(8,128)(2,1)S(1)}, bf16[32,3584]{1,0:T(8,128)(2,1)}, u32[]{:S(2)}) copy-start(bf16[32,3584]{1,0:T(8,128)(2,1)} %param.9) | copy-start | bytes 688132
  7.2 97.1 %reduce-scatter.4.cloned.1.call-start = ((), (), s32[]{:S(2)}) async-start(), calls=%async_computation.2 | async-start | bytes 786432 | tf_op jit(solution)/shard_map/reduce_scatter | solution.py:112
  7.2 9.4 %collective-permute-start = (bf16[32,3584]{1,0:T(8,128)(2,1)}, bf16[32,3584]{1,0:T(8,128)(2,1)S(1)}, u32[]{:S(2)}, u32[]{:S(2)}) collective-permute-start(bf16[32,3584]{1,0:T(8,128)(2,1)} %param.9), channel_id=1, source_target_pairs={{0,2},{2,4},{4,6},{6,8},{8,10},{10,12},{12,14},{14,16},{16,18},{18... | collective-permute-start | bytes 688136 | tf_op jit(solution)/shard_map/ppermute | solution.py:101
  16.7 8.1 %collective-permute-start.1 = (bf16[32,3584]{1,0:T(8,128)(2,1)S(1)}, bf16[32,3584]{1,0:T(8,128)(2,1)S(1)}, u32[]{:S(2)}, u32[]{:S(2)}) collective-permute-start(bf16[32,3584]{1,0:T(8,128)(2,1)S(1)} %collective-permute-done), channel_id=1, source_target_pairs={{0,2},{2,4},{4,6},{6,8},{8,10},{10,12},{12,14},{14,16},{16,18},{18... | collective-permute-start | bytes 688136 | tf_op jit(solution)/shard_map/ppermute | solution.py:101
  16.7 8.3 %collective-permute-start.8 = (bf16[32,3584]{1,0:T(8,128)(2,1)}, bf16[32,3584]{1,0:T(8,128)(2,1)S(1)}, u32[]{:S(2)}, u32[]{:S(2)}) collective-permute-start(bf16[32,3584]{1,0:T(8,128)(2,1)} %param.9), channel_id=1, source_target_pairs={{0,30},{2,0},{4,2},{6,4},{8,6},{10,8},{12,10},{14,12},{16,14},{18,... | collective-permute-start | bytes 688136 | tf_op jit(solution)/shard_map/ppermute | solution.py:104
  24.8 8.2 %collective-permute-start.2 = (bf16[32,3584]{1,0:T(8,128)(2,1)S(1)}, bf16[32,3584]{1,0:T(8,128)(2,1)S(1)}, u32[]{:S(2)}, u32[]{:S(2)}) collective-permute-start(bf16[32,3584]{1,0:T(8,128)(2,1)S(1)} %collective-permute-done.1), channel_id=1, source_target_pairs={{0,2},{2,4},{4,6},{6,8},{8,10},{10,12},{12,14},{14,16},{16,18},{18... | collective-permute-start | bytes 688136 | tf_op jit(solution)/shard_map/ppermute | solution.py:101
  25.0 8.1 %collective-permute-start.9 = (bf16[32,3584]{1,0:T(8,128)(2,1)S(1)}, bf16[32,3584]{1,0:T(8,128)(2,1)S(1)}, u32[]{:S(2)}, u32[]{:S(2)}) collective-permute-start(bf16[32,3584]{1,0:T(8,128)(2,1)S(1)} %collective-permute-done.8), channel_id=1, source_target_pairs={{0,30},{2,0},{4,2},{6,4},{8,6},{10,8},{12,10},{14,12},{16,14},{18,... | collective-permute-start | bytes 688136 | tf_op jit(solution)/shard_map/ppermute | solution.py:104
  33.1 8.2 %collective-permute-start.3 = (bf16[32,3584]{1,0:T(8,128)(2,1)S(1)}, bf16[32,3584]{1,0:T(8,128)(2,1)S(1)}, u32[]{:S(2)}, u32[]{:S(2)}) collective-permute-start(bf16[32,3584]{1,0:T(8,128)(2,1)S(1)} %collective-permute-done.2), channel_id=1, source_target_pairs={{0,2},{2,4},{4,6},{6,8},{8,10},{10,12},{12,14},{14,16},{16,18},{18... | collective-permute-start | bytes 688136 | tf_op jit(solution)/shard_map/ppermute | solution.py:101
  33.1 8.2 %collective-permute-start.10 = (bf16[32,3584]{1,0:T(8,128)(2,1)S(1)}, bf16[32,3584]{1,0:T(8,128)(2,1)S(1)}, u32[]{:S(2)}, u32[]{:S(2)}) collective-permute-start(bf16[32,3584]{1,0:T(8,128)(2,1)S(1)} %collective-permute-done.9), channel_id=1, source_target_pairs={{0,30},{2,0},{4,2},{6,4},{8,6},{10,8},{12,10},{14,12},{16,14},{18,... | collective-permute-start | bytes 688136 | tf_op jit(solution)/shard_map/ppermute | solution.py:104
  41.3 8.2 %collective-permute-start.4 = (bf16[32,3584]{1,0:T(8,128)(2,1)S(1)}, bf16[32,3584]{1,0:T(8,128)(2,1)S(1)}, u32[]{:S(2)}, u32[]{:S(2)}) collective-permute-start(bf16[32,3584]{1,0:T(8,128)(2,1)S(1)} %collective-permute-done.3), channel_id=1, source_target_pairs={{0,2},{2,4},{4,6},{6,8},{8,10},{10,12},{12,14},{14,16},{16,18},{18... | collective-permute-start | bytes 688136 | tf_op jit(solution)/shard_map/ppermute | solution.py:101
  41.4 9.3 %collective-permute-start.11 = (bf16[32,3584]{1,0:T(8,128)(2,1)S(1)}, bf16[32,3584]{1,0:T(8,128)(2,1)S(1)}, u32[]{:S(2)}, u32[]{:S(2)}) collective-permute-start(bf16[32,3584]{1,0:T(8,128)(2,1)S(1)} %collective-permute-done.10), channel_id=1, source_target_pairs={{0,30},{2,0},{4,2},{6,4},{8,6},{10,8},{12,10},{14,12},{16,14},{18,... | collective-permute-start | bytes 688136 | tf_op jit(solution)/shard_map/ppermute | solution.py:104
  49.6 8.3 %copy-start.4 = (bf16[32,3584]{1,0:T(8,128)(2,1)}, bf16[32,3584]{1,0:T(8,128)(2,1)S(1)}, u32[]{:S(2)}) copy-start(bf16[32,3584]{1,0:T(8,128)(2,1)S(1)} %collective-permute-done.4) | copy-start | bytes 688132
  49.6 8.3 %collective-permute-start.5 = (bf16[32,3584]{1,0:T(8,128)(2,1)S(1)}, bf16[32,3584]{1,0:T(8,128)(2,1)}, u32[]{:S(2)}, u32[]{:S(2)}) collective-permute-start(bf16[32,3584]{1,0:T(8,128)(2,1)S(1)} %collective-permute-done.4), channel_id=1, source_target_pairs={{0,2},{2,4},{4,6},{6,8},{8,10},{10,12},{12,14},{14,16},{16,18},{18... | collective-permute-start | bytes 688136 | tf_op jit(solution)/shard_map/ppermute | solution.py:101
  50.7 9.4 %collective-permute-start.12 = (bf16[32,3584]{1,0:T(8,128)(2,1)S(1)}, bf16[32,3584]{1,0:T(8,128)(2,1)}, u32[]{:S(2)}, u32[]{:S(2)}) collective-permute-start(bf16[32,3584]{1,0:T(8,128)(2,1)S(1)} %collective-permute-done.11), channel_id=1, source_target_pairs={{0,30},{2,0},{4,2},{6,4},{8,6},{10,8},{12,10},{14,12},{16,14},{18,... | collective-permute-start | bytes 688136 | tf_op jit(solution)/shard_map/ppermute | solution.py:104
  57.9 8.5 %collective-permute-start.6 = (bf16[32,3584]{1,0:T(8,128)(2,1)}, bf16[32,3584]{1,0:T(8,128)(2,1)}, u32[]{:S(2)}, u32[]{:S(2)}) collective-permute-start(bf16[32,3584]{1,0:T(8,128)(2,1)} %collective-permute-done.5), channel_id=1, source_target_pairs={{0,2},{2,4},{4,6},{6,8},{8,10},{10,12},{12,14},{14,16},{16,18},{18... | collective-permute-start | bytes 688136 | tf_op jit(solution)/shard_map/ppermute | solution.py:101
  59.2 25.4 %copy-start.5 = (bf16[32,3584]{1,0:T(8,128)(2,1)S(1)}, bf16[32,3584]{1,0:T(8,128)(2,1)}, u32[]{:S(2)}) copy-start(bf16[32,3584]{1,0:T(8,128)(2,1)} %copy-done.4) | copy-start | bytes 688132
  60.1 8.5 %collective-permute-start.13 = (bf16[32,3584]{1,0:T(8,128)(2,1)}, bf16[32,3584]{1,0:T(8,128)(2,1)}, u32[]{:S(2)}, u32[]{:S(2)}) collective-permute-start(bf16[32,3584]{1,0:T(8,128)(2,1)} %collective-permute-done.12), channel_id=1, source_target_pairs={{0,30},{2,0},{4,2},{6,4},{8,6},{10,8},{12,10},{14,12},{16,14},{18,... | collective-permute-start | bytes 688136 | tf_op jit(solution)/shard_map/ppermute | solution.py:104
  66.4 8.5 %collective-permute-start.7 = (bf16[32,3584]{1,0:T(8,128)(2,1)}, bf16[32,3584]{1,0:T(8,128)(2,1)}, u32[]{:S(2)}, u32[]{:S(2)}) collective-permute-start(bf16[32,3584]{1,0:T(8,128)(2,1)} %collective-permute-done.6), channel_id=1, source_target_pairs={{0,2},{2,4},{4,6},{6,8},{8,10},{10,12},{12,14},{14,16},{16,18},{18... | collective-permute-start | bytes 688136 | tf_op jit(solution)/shard_map/ppermute | solution.py:101
  68.6 21.2 %copy-start.10 = (f32[256,3584]{1,0:T(8,128)S(1)}, f32[256,3584]{1,0:T(8,128)}, u32[]{:S(2)}) copy-start(f32[256,3584]{1,0:T(8,128)} %param.10) | copy-start | bytes 11010052
  68.6 13.1 %collective-permute-start.14 = (bf16[32,3584]{1,0:T(8,128)(2,1)}, bf16[32,3584]{1,0:T(8,128)(2,1)S(1)}, u32[]{:S(2)}, u32[]{:S(2)}) collective-permute-start(bf16[32,3584]{1,0:T(8,128)(2,1)} %collective-permute-done.13), channel_id=1, source_target_pairs={{0,30},{2,0},{4,2},{6,4},{8,6},{10,8},{12,10},{14,12},{16,14},{18,... | collective-permute-start | bytes 688136 | tf_op jit(solution)/shard_map/ppermute | solution.py:104
  84.8 7.5 %copy-start.7 = (bf16[256,64]{0,1:T(8,128)(2,1)S(1)}, bf16[256,64]{0,1:T(8,128)(2,1)}, u32[]{:S(2)}) copy-start(bf16[256,64]{0,1:T(8,128)(2,1)} %param.15) | copy-start | bytes 98308
  86.8 18.6 %copy-start.6 = (bf16[256,2,128]{0,2,1:T(8,128)(2,1)S(1)}, bf16[256,2,128]{0,2,1:T(8,128)(2,1)}, u32[]{:S(2)}) copy-start(bf16[256,2,128]{0,2,1:T(8,128)(2,1)} %copy.108) | copy-start | bytes 393220
  86.9 3.0 %copy-start.1 = (bf16[1024,3584]{1,0:T(8,128)(2,1)}, bf16[1024,3584]{1,0:T(8,128)(2,1)S(1)}, u32[]{:S(2)}) copy-start(bf16[1024,3584]{1,0:T(8,128)(2,1)S(1)} %constant_dynamic-update-slice_fusion) | copy-start | bytes 22020100
  91.8 14.8 %copy-start.2 = (bf16[256,512]{1,0:T(8,128)(2,1)S(1)}, bf16[256,512]{1,0:T(8,128)(2,1)}, u32[]{:S(2)}) copy-start(bf16[256,512]{1,0:T(8,128)(2,1)} %param.14) | copy-start | bytes 786436
  91.8 121.7 %all-reduce.4.cloned.1.call-start = ((), (), s32[]{:S(2)}) async-start(), calls=%async_computation.4 | async-start | bytes 1310720
  106.5 54.3 %copy-start.8 = (f32[3584]{0:T(1024)S(1)}, f32[3584]{0:T(1024)}, u32[]{:S(2)}) copy-start(f32[3584]{0:T(1024)} %param.12) | copy-start | bytes 43012
  106.5 54.4 %copy-start.9 = (f32[256]{0:T(256)S(1)}, f32[256]{0:T(256)}, u32[]{:S(2)}) copy-start(f32[256]{0:T(256)} %param.11) | copy-start | bytes 3076
  109.4 114.4 %reduce-scatter.6.cloned.1.call-start = ((), (), s32[]{:S(2)}) async-start(), calls=%async_computation.3 | async-start | bytes 1572864 | tf_op jit(solution)/shard_map/reduce_scatter | solution.py:131
Sparse Core Ops, SparseCore 0:
  91.9 12.3 reduce-scatter.3
  109.5 91.8 all-reduce.3
  203.6 20.1 reduce-scatter.5
